TPU v7x, 256 devices: a whole 4x4x8 slice. The times are simulated.
256 devices in a mesh: depth: 16 (over x, y), tile: 16 (over z, core).
Axes of the slice: x: 4, y: 4, z: 8, core: 2. Of those that a mesh axis runs over, the one named last changes fastest.
Arguments:
- density: float32 [512, 512, 2048], P('depth', 'tile'), may hold values from 0 to 1
- palette: float32 [2, 3], replicated, may hold values from 0.2 to 1
- light_dir: float32 [2, 3], replicated, may hold values from -4 to 4
- slab_of: int32 [16], replicated, may hold values from 0 to 15, each once
Outputs:
- images: float32 [2, 4, 512, 2048], P(None, None, 'tile', 'depth')
Inputs may be any that keep to these rules, and one draw needn't show every extreme that they name: `slab_of`: each of 0 to 15 appears once.
All inputs are finite; a program needn't handle non-finite values.
Results may differ from a plain program's by a relative error of at most 0.0008.
Values may be sent and summed in bfloat16 or wider, within the bound.
No kernel may reach another device: no remote copies, remote signals or barrier semaphores. Data moves between devices by JAX's collectives and lax.ppermute only.
A program may use at most 128 MiB of HBM per device.

v0:
```python
import jax
import jax.numpy as jnp
from jax import lax
from jax.sharding import PartitionSpec as P

HIGH = lax.Precision.HIGHEST


def padded_2(block, sides, width):
    for axis, dim in sides:
        count = lax.axis_size(axis)
        forward = [(i, i + 1) for i in range(count - 1)]
        backward = [(target, source) for source, target in forward]
        low = lax.ppermute(
            lax.slice_in_dim(block, block.shape[dim] - width, None, axis=dim), axis, forward
        )
        high = lax.ppermute(lax.slice_in_dim(block, 0, width, axis=dim), axis, backward)
        block = jnp.concatenate([low, block, high], axis=dim)
    return block


def centred(field, axis):
    size = field.shape[axis]
    upper = jnp.concatenate(
        [
            lax.slice_in_dim(field, 1, size, axis=axis),
            lax.slice_in_dim(field, size - 1, size, axis=axis),
        ],
        axis,
    )
    lower = jnp.concatenate(
        [lax.slice_in_dim(field, 0, 1, axis=axis), lax.slice_in_dim(field, 0, size - 1, axis=axis)],
        axis,
    )
    return (upper - lower) * 0.5


def march(block, grad_x, palette, light_dir, factor):
    grad_z = centred(block, 0)
    grad_y = centred(block, 2)
    length = jnp.sqrt(grad_x * grad_x + grad_y * grad_y + grad_z * grad_z + 0.25)
    optical = block * factor
    opacity = 1.0 - jnp.exp(-optical)
    running = jnp.cumsum(optical, axis=0)
    slab_tau = running[-1]
    before = [running - optical, slab_tau[None] - running]
    colours = []
    for view in range(2):
        facing = (
            grad_x * light_dir[view, 0] + grad_y * light_dir[view, 1] + grad_z * light_dir[view, 2]
        )
        shade = 0.3 + jnp.abs(facing) / length
        weight = opacity * jnp.exp(-before[view]) * shade
        plain = jnp.sum(weight, axis=0)
        dense = jnp.sum(block * weight, axis=0)
        colours.append(
            palette[0][:, None, None] * plain[None] + palette[1][:, None, None] * dense[None]
        )
    return (jnp.stack(colours).astype(jnp.bfloat16), slab_tau.astype(jnp.bfloat16))


def on_device(density, palette, light_dir, slab_of):
    slab_rows, tile_rows, image_cols = density.shape
    depth_count = lax.axis_size("depth")
    tile_count = lax.axis_size("tile")
    tile_place = lax.axis_index("tile")
    depth_place = lax.axis_index("depth")
    padded = padded_2(density, (("tile", 1),), 1)
    left_plane = jnp.where(tile_place == 0, density[:, :1], padded[:, :1])
    right_plane = jnp.where(tile_place == tile_count - 1, density[:, -1:], padded[:, -1:])
    full_x = jnp.concatenate([left_plane, density, right_plane], axis=1)
    grad_x = (full_x[:, 2:] - full_x[:, :-2]) * 0.5
    factor = 3.0 / (slab_rows * depth_count)
    slab_rgb, slab_tau = march(density, grad_x, palette, light_dir, factor)
    piece_width = image_cols // depth_count
    my_slab = slab_of[depth_place]
    earlier = (slab_of < my_slab).astype(jnp.float32)
    later = (slab_of > my_slab).astype(jnp.float32)
    tau_full = lax.all_gather(slab_tau[None], "depth", axis=0, tiled=True).astype(jnp.float32)
    front_one = jnp.einsum("k,kxy->xy", earlier, tau_full, precision=HIGH)
    front_two = jnp.einsum("k,kxy->xy", later, tau_full, precision=HIGH)
    total = jnp.sum(tau_full, axis=0)
    fading = jnp.exp(-jnp.stack([front_one, front_two]))
    terms = slab_rgb.astype(jnp.float32) * fading[:, None]
    colours = lax.psum_scatter(terms, "depth", scatter_dimension=3, tiled=True)
    coverage = lax.dynamic_slice_in_dim(
        1.0 - jnp.exp(-total), depth_place * piece_width, piece_width, 1
    )
    coverage = jnp.broadcast_to(coverage[None, None], (2, 1, tile_rows, piece_width))
    return jnp.concatenate([colours, coverage], axis=1)


def solution(mesh):
    in_specs = (P("depth", "tile", None), P(), P(), P())
    out_specs = P(None, None, "tile", "depth")
    return jax.shard_map(
        on_device, mesh=mesh, in_specs=in_specs, out_specs=out_specs, check_vma=False
    )
```

profile of v0, /device:TPU:2, one launch (start us, length us, event | category | flops | bytes accessed | tf_op | source)
XLA Modules:
  0.0 228.3 jit_solution(13227945402182114814)
XLA Ops:
  6.5 0.0 all-gather.2.cloned.1.call-start
  6.5 2.7 %fusion.23 = (f32[32,1,2048]{2,1,0:T(1,128)S(1)}, f32[32,1,2048]{2,1,0:T(1,128)S(1)}) fusion(f32[32,32,2048]{2,1,0:T(8,128)} %param.4), kind=kLoop, calls=%fused_computation.46 | loop fusion | bytes 1048576 | tf_op jit(solution)/shard_map/slice | solution.py:69
  9.2 1.3 collective-permute-start
  10.5 3.0 %collective-permute-start.1 = (f32[32,1,2048]{2,1,0:T(1,128)S(1)}, f32[32,1,2048]{2,1,0:T(1,128)S(1)}, u32[]{:S(2)}, u32[]{:S(2)}) collective-permute-start(f32[32,1,2048]{2,1,0:T(1,128)S(1)} %get-tuple-element.20), channel_id=1, source_target_pairs={{0,1},{1,2},{2,3},{3,4},{4,5},{5,6},{6,7},{7,8},{8,9},{9,10},{10,1... | collective-permute-start | bytes 786440 | tf_op jit(solution)/shard_map/ppermute | solution.py:14
  13.6 0.0 slice-start
  13.6 1.2 fusion.22
  14.8 0.0 slice-start.1
  14.8 11.5 %fusion.21 = (f32[31,32,2048]{2,1,0:T(8,128)}, f32[31,32,2048]{2,1,0:T(8,128)}) fusion(f32[32,32,2048]{2,1,0:T(8,128)} %param.4), kind=kLoop, calls=%fused_computation.44 | loop fusion | bytes 32505856 | tf_op jit(solution)/shard_map/slice | solution.py:26
  26.3 0.0 slice-done
  26.3 0.0 slice-done.1
  26.3 0.0 copy-start.3
  26.3 0.0 copy-start.1
  26.4 0.0 copy-start.2
  26.4 7.3 %fusion.19 = (f32[32,32,2047]{2,1,0:T(8,128)}, f32[32,32,2047]{2,1,0:T(8,128)}) fusion(f32[32,32,2048]{2,1,0:T(8,128)S(1)} %bitcast.22), kind=kLoop, calls=%fused_computation.42 | loop fusion | bytes 33538048 | tf_op jit(solution)/shard_map/slice | solution.py:26
  33.6 0.0 copy-done.3
  33.7 0.0 copy-done.1
  33.7 0.7 fusion.24
  38.1 0.0 copy-done.2
  38.1 0.7 dynamic_slice.6
  38.8 1.4 fusion.20
  40.2 0.0 collective-permute-done
  40.2 0.0 collective-permute-done.1
  40.2 2.9 %broadcast_select_fusion.1 = (f32[32,1,2048]{2,1,0:T(1,128)S(1)}, f32[32,1,2048]{2,1,0:T(1,128)S(1)}) fusion(f32[32,1,2048]{2,1,0:T(1,128)S(1)} %collective-permute-done, pred[]{:T(512)S(6)} %eq.6, f32[32,32,2048]{2,1,0:T(8,128)} %param.4, f32[32,1,2048]{2,1,0:T(1,128)S(1)} %collective-permute-done.1, pred[]{:T(512)S(6)} %eq.7), kind=kLoop, calls=%fused_computation.25 | loop fusion | flops 131072 | bytes 1572866 | tf_op jit(solution)/shard_map/jit(_where)/select_n | solution.py:70
  43.1 30.5 %add_multiply_fusion.1 = (f32[32,32,2048]{2,1,0:T(8,128)}, f32[32,32,2048]{2,1,0:T(8,128)}) fusion(f32[32,32,2048]{2,1,0:T(8,128)} %param.4, f32[32,1,2048]{2,1,0:T(1,128)S(1)} %get-tuple-element.18, f32[32,1,2048]{2,1,0:T(1,128)S(1)} %get-tuple-element.17, f32[]{:T(128)} %bitcast.3, f32[]{:T(128)} %bitcast.2, f32[]{:T(128)} %bitcast.1, ...), kind=kOutput, calls=%fused_computation.8 | output fusion | flops 136314880 | bytes 59244556 | tf_op jit(solution)/shard_map/jit(cumsum)/reduce_window_sum | solution.py:44
  73.6 1.6 slice.97
  75.2 1.0 slice_bitcast_fusion
  76.2 0.0 all-gather.2.cloned.1.call-update
  76.2 0.2 reduce-scatter.2.cloned.1.call-start
  76.5 31.7 %fusion.18 = (f32[32,2048]{1,0:T(8,128)S(1)}, f32[32,2048]{1,0:T(8,128)S(1)}, f32[32,2048]{1,0:T(8,128)S(1)}, f32[32,2048]{1,0:T(8,128)S(1)}) fusion(f32[32,32,2048]{2,1,0:T(8,128)} %get-tuple-element.31, f32[32,32,2048]{2,1,0:T(8,128)} %param.4, f32[]{:T(128)} %bitcast.8, f32[31,32,2048]{2,1,0:T(8,128)} %get-tuple-element.14, ...), kind=kLoop, calls=%fused_computation.41 | loop fusion | flops 81526784 | bytes 60555276 | tf_op jit(solution)/shard_map/reduce_sum | solution.py:54
  108.2 0.3 add_convert_fusion.1
  108.5 21.2 %all-gather.2.cloned.1.call-done = bf16[16,32,2048]{2,1,0:T(8,128)(2,1)} async-done(((bf16[1,32,2048]{2,1,0:T(8,128)(2,1)}), bf16[16,32,2048]{2,1,0:T(8,128)(2,1)}) %all-gather.2.cloned.1.call-update) | async-done | bytes 2097168 | tf_op jit(solution)/shard_map/all_gather | solution.py:79
  129.6 0.0 copy-start
  129.6 4.8 %fusion.4 = f32[1,32,2048]{2,0,1:T(1,128)S(1)} fusion(bf16[16,32,2048]{2,1,0:T(8,128)(2,1)} %all-gather.2.cloned.1.call-done, s32[16]{0:T(128)S(1)} %copy-done.2, s32[]{:T(128)} %bitcast.9), kind=kOutput, calls=%fused_computation.15 | convolution fusion | flops 2097168 | bytes 2359364 | tf_op jit(solution)/shard_map/k,kxy->xy/dot_general | solution.py:81
  134.5 0.1 copy.7
  134.5 4.7 %fusion.6 = f32[1,32,2048]{2,0,1:T(1,128)S(1)} fusion(bf16[16,32,2048]{2,1,0:T(8,128)(2,1)} %all-gather.2.cloned.1.call-done, s32[16]{0:T(128)S(1)} %copy-done.2, s32[]{:T(128)} %bitcast.9), kind=kOutput, calls=%fused_computation.17 | convolution fusion | flops 2097168 | bytes 2359364 | tf_op jit(solution)/shard_map/k,kxy->xy/dot_general | solution.py:80
  139.2 0.1 copy.6
  139.3 0.1 fusion.8
  139.4 1.3 convert_multiply_fusion
  140.7 0.0 reduce-scatter.2.cloned.1.call-update
  140.7 0.0 copy-done
  140.7 0.4 convert_reduce_fusion
  141.1 78.8 %reduce-scatter.2.cloned.1.call-done = f32[2,3,32,128]{3,2,1,0:T(8,128)} async-done(((f32[2,3,32,2048]{3,2,1,0:T(8,128)}), f32[2,3,32,128]{3,2,1,0:T(8,128)}) %reduce-scatter.2.cloned.1.call-update) | async-done | bytes 98320 | tf_op jit(solution)/shard_map/reduce_scatter | solution.py:85
  219.9 1.6 pad_maximum_fusion.2
  (4 shorter events, 0.0 us)
Async XLA Ops:
  6.5 123.1 %all-gather.2.cloned.1.call-start = ((), (), s32[]{:S(2)}) async-start(), calls=%async_computation.1 | async-start | bytes 2228224 | tf_op jit(solution)/shard_map/all_gather | solution.py:79
  9.2 31.0 %collective-permute-start = (f32[32,1,2048]{2,1,0:T(1,128)S(1)}, f32[32,1,2048]{2,1,0:T(1,128)S(1)}, u32[]{:S(2)}, u32[]{:S(2)}) collective-permute-start(f32[32,1,2048]{2,1,0:T(1,128)S(1)} %get-tuple-element.19), channel_id=1, source_target_pairs={{1,0},{2,1},{3,2},{4,3},{5,4},{6,5},{7,6},{8,7},{9,8},{10,9},{11,1... | collective-permute-start | bytes 786440 | tf_op jit(solution)/shard_map/ppermute | solution.py:17
  10.5 29.7 %collective-permute-start.1 = (f32[32,1,2048]{2,1,0:T(1,128)S(1)}, f32[32,1,2048]{2,1,0:T(1,128)S(1)}, u32[]{:S(2)}, u32[]{:S(2)}) collective-permute-start(f32[32,1,2048]{2,1,0:T(1,128)S(1)} %get-tuple-element.20), channel_id=1, source_target_pairs={{0,1},{1,2},{2,3},{3,4},{4,5},{5,6},{6,7},{7,8},{8,9},{9,10},{10,1... | collective-permute-start | bytes 786440 | tf_op jit(solution)/shard_map/ppermute | solution.py:14
  13.6 12.8 %slice-start = ((s8[8388608]{0:T(1024)(128)(4,1)}), s8[4194304]{0:T(1024)(128)(4,1)S(1)}, s32[]{:S(2)}) async-start(s8[8388608]{0:T(1024)(128)(4,1)} %bitcast.21), calls=%async_computation.3 | async-start | bytes 8388608
  14.8 11.5 %slice-start.1 = ((s8[8388608]{0:T(1024)(128)(4,1)}), s8[4194304]{0:T(1024)(128)(4,1)S(1)}, s32[]{:S(2)}) async-start(s8[8388608]{0:T(1024)(128)(4,1)} %bitcast.21), calls=%async_computation.4 | async-start | bytes 8388608
  26.3 7.3 %copy-start.3 = (f32[2,3]{1,0:T(2,128)S(1)}, f32[2,3]{1,0:T(2,128)}, u32[]{:S(2)}) copy-start(f32[2,3]{1,0:T(2,128)} %param.5) | copy-start | bytes 76
  26.3 7.3 %copy-start.1 = (f32[2,3]{1,0:T(2,128)S(1)}, f32[2,3]{1,0:T(2,128)}, u32[]{:S(2)}) copy-start(f32[2,3]{1,0:T(2,128)} %param.6) | copy-start | bytes 76
  26.4 11.8 %copy-start.2 = (s32[16]{0:T(128)S(1)}, s32[16]{0:T(128)}, u32[]{:S(2)}) copy-start(s32[16]{0:T(128)} %param.7) | copy-start | bytes 196
  76.2 143.6 %reduce-scatter.2.cloned.1.call-start = ((), (), s32[]{:S(2)}) async-start(), calls=%async_computation.2 | async-start | bytes 1671168 | tf_op jit(solution)/shard_map/reduce_scatter | solution.py:85
  129.6 11.1 %copy-start = (bf16[16,32,2048]{2,1,0:T(8,128)(2,1)S(1)}, bf16[16,32,2048]{2,1,0:T(8,128)(2,1)}, u32[]{:S(2)}) copy-start(bf16[16,32,2048]{2,1,0:T(8,128)(2,1)} %all-gather.2.cloned.1.call-done) | copy-start | bytes 6291460
Sparse Core Ops, SparseCore 0:
  76.4 53.2 all-gather.1
  140.8 79.0 reduce-scatter.1
where the time goes:
time: 229 us; the launch traced here: 228 us
  waiting for transfers between devices  100 us (44%)
  other arithmetic  68.7 us (30%)
  local copies, waits for them, and re-layouts  28.2 us (12%)
  between operations  17.4 us (8%)
  matrix products  9.46 us (4%)
  starting transfers between devices  4.56 us (2%)
    reduce_scatter x1, waiting for transfers between devices, on_device(): colours = lax.psum_scatter(terms, 'depth', scatter_dimension=3, tiled=True)  78.8 us
    reduce_sum x1, other arithmetic, march(): plain = jnp.sum(weight, axis=0)  31.7 us
    another operation x1, other arithmetic, march(): running = jnp.cumsum(optical, axis=0)  30.5 us
    all_gather x1, waiting for transfers between devices, on_device(): lax.all_gather(slab_tau[None], 'depth', axis=0, tiled=True)  21.2 us
    slice x2, local copies, waits for them, and re-layouts, centred(): lax.slice_in_dim(field, 1, size, axis=axis)  18.8 us
    dot_general x1, matrix products, on_device(): front_two = jnp.einsum('k,kxy->xy', later, tau_full, precision=HIGH)  4.8 us
    dot_general x1, matrix products, on_device(): front_one = jnp.einsum('k,kxy->xy', earlier, tau_full, precision=HIGH)  4.65 us
  transfers between devices with their start and end apart: 4, of which 2 were waited for; matrix products, arithmetic and copies ran while one was open for 24% of the time, Pallas kernels for 0%

commit v1 on v0

--- a/solution.py
+++ b/solution.py
@@ -76,7 +76,15 @@
     my_slab = slab_of[depth_place]
     earlier = (slab_of < my_slab).astype(jnp.float32)
     later = (slab_of > my_slab).astype(jnp.float32)
-    tau_full = lax.all_gather(slab_tau[None], "depth", axis=0, tiled=True).astype(jnp.float32)
+    tau_full = jnp.concatenate(
+        lax.all_to_all(
+            jnp.stack(lax.axis_size("depth") * [slab_tau[None]], 0),
+            axis_name="depth",
+            split_axis=0,
+            concat_axis=0,
+        ),
+        0,
+    ).astype(jnp.float32)
     front_one = jnp.einsum("k,kxy->xy", earlier, tau_full, precision=HIGH)
     front_two = jnp.einsum("k,kxy->xy", later, tau_full, precision=HIGH)
     total = jnp.sum(tau_full, axis=0)

time: 229 us -> 217 us (0.948)
  waiting for transfers between devices: 100 us -> 81.8 us
  starting transfers between devices: 4.56 us -> 12 us
  matrix products: 9.46 us -> 6 us
    all_gather x1 -> x0, waiting for transfers between devices: 21.2 us -> none  [on_device(): lax.all_gather(slab_tau[None], 'depth', axis=0, tiled=True)]
    all_to_all x0 -> x1, starting transfers between devices: none -> 7.48 us  [on_device(): lax.all_to_all(jnp.stack(lax.axis_size('depth') * [slab_tau[None]], 0), a...]
    reduce_scatter x1, waiting for transfers between devices: 78.8 us -> 81.8 us  [on_device(): colours = lax.psum_scatter(terms, 'depth', scatter_dimension=3, tiled=True)]
  transfers between devices with their start and end apart: 4 -> 4, of which waited for: 2 -> 1; matrix products, arithmetic and copies ran while one was open for 24% -> 26% of each run, Pallas kernels for 0% -> 0%
where the time goes in v1:
time: 217 us; the launch traced here: 216 us
  waiting for transfers between devices  81.8 us (38%)
  other arithmetic  69.2 us (32%)
  local copies, waits for them, and re-layouts  29.9 us (14%)
  between operations  17.5 us (8%)
  starting transfers between devices  12 us (6%)
  matrix products  6 us (3%)
    reduce_scatter x1, waiting for transfers between devices, on_device(): colours = lax.psum_scatter(terms, 'depth', scatter_dimension=3, tiled=True)  81.8 us
    reduce_sum x1, other arithmetic, march(): plain = jnp.sum(weight, axis=0)  32 us
    another operation x1, other arithmetic, march(): running = jnp.cumsum(optical, axis=0)  30.6 us
    slice x2, local copies, waits for them, and re-layouts, centred(): lax.slice_in_dim(field, 1, size, axis=axis)  18.9 us
    all_to_all x1, starting transfers between devices, on_device(): lax.all_to_all(jnp.stack(lax.axis_size('depth') * [slab_tau[None]], 0), a...  7.48 us
  transfers between devices with their start and end apart: 4, of which 1 were waited for; matrix products, arithmetic and copies ran while one was open for 26% of the time, Pallas kernels for 0%

profile of v1, /device:TPU:2, one launch (start us, length us, event | category | flops | bytes accessed | tf_op | source)
XLA Modules:
  0.0 216.4 jit_solution(13220744459441400342)
XLA Ops:
  6.5 2.7 %fusion.24 = (f32[32,1,2048]{2,1,0:T(1,128)S(1)}, f32[32,1,2048]{2,1,0:T(1,128)S(1)}) fusion(f32[32,32,2048]{2,1,0:T(8,128)} %param.4), kind=kLoop, calls=%fused_computation.47 | loop fusion | bytes 1048576 | tf_op jit(solution)/shard_map/slice | solution.py:69
  9.2 1.3 collective-permute-start
  10.5 3.0 %collective-permute-start.1 = (f32[32,1,2048]{2,1,0:T(1,128)S(1)}, f32[32,1,2048]{2,1,0:T(1,128)S(1)}, u32[]{:S(2)}, u32[]{:S(2)}) collective-permute-start(f32[32,1,2048]{2,1,0:T(1,128)S(1)} %get-tuple-element.20), channel_id=1, source_target_pairs={{0,1},{1,2},{2,3},{3,4},{4,5},{5,6},{6,7},{7,8},{8,9},{9,10},{10,1... | collective-permute-start | bytes 786440 | tf_op jit(solution)/shard_map/ppermute | solution.py:14
  13.6 0.0 slice-start
  13.6 1.2 fusion.23
  14.8 0.0 copy-start
  14.8 0.0 slice-start.1
  14.8 11.6 %fusion.22 = (f32[31,32,2048]{2,1,0:T(8,128)}, f32[31,32,2048]{2,1,0:T(8,128)}) fusion(f32[32,32,2048]{2,1,0:T(8,128)} %param.4), kind=kLoop, calls=%fused_computation.45 | loop fusion | bytes 32505856 | tf_op jit(solution)/shard_map/slice | solution.py:26
  26.4 0.0 slice-done
  26.4 0.0 slice-done.1
  26.4 0.0 copy-start.5
  26.4 0.0 copy-start.3
  26.4 0.0 copy-start.4
  26.5 7.3 %fusion.20 = (f32[32,32,2047]{2,1,0:T(8,128)}, f32[32,32,2047]{2,1,0:T(8,128)}) fusion(f32[32,32,2048]{2,1,0:T(8,128)S(1)} %bitcast.26), kind=kLoop, calls=%fused_computation.43 | loop fusion | bytes 33538048 | tf_op jit(solution)/shard_map/slice | solution.py:26
  33.7 0.0 copy-done.5
  33.7 0.0 copy-done.3
  33.7 0.7 fusion.25
  38.3 0.0 copy-done.4
  38.3 0.6 dynamic_slice.6
  39.0 1.4 fusion.21
  40.4 0.0 collective-permute-done
  40.4 0.0 collective-permute-done.1
  40.4 2.9 %broadcast_select_fusion.1 = (f32[32,1,2048]{2,1,0:T(1,128)S(1)}, f32[32,1,2048]{2,1,0:T(1,128)S(1)}) fusion(f32[32,1,2048]{2,1,0:T(1,128)S(1)} %collective-permute-done, pred[]{:T(512)S(6)} %eq.6, f32[32,32,2048]{2,1,0:T(8,128)} %param.4, f32[32,1,2048]{2,1,0:T(1,128)S(1)} %collective-permute-done.1, pred[]{:T(512)S(6)} %eq.7), kind=kLoop, calls=%fused_computation.25 | loop fusion | flops 131072 | bytes 1572866 | tf_op jit(solution)/shard_map/jit(_where)/select_n | solution.py:70
  43.3 0.0 copy-start.1
  43.3 0.0 copy-start.2
  43.3 0.0 copy-done
  43.3 30.6 %add_multiply_fusion.1 = (f32[32,32,2048]{2,1,0:T(8,128)}, f32[32,32,2048]{2,1,0:T(8,128)}) fusion(f32[32,32,2048]{2,1,0:T(8,128)} %param.4, f32[32,1,2048]{2,1,0:T(1,128)S(1)} %get-tuple-element.18, f32[32,1,2048]{2,1,0:T(1,128)S(1)} %get-tuple-element.17, f32[]{:T(128)} %bitcast.3, f32[]{:T(128)} %bitcast.2, f32[]{:T(128)} %bitcast.1, ...), kind=kOutput, calls=%fused_computation.8 | output fusion | flops 136314880 | bytes 59244556 | tf_op jit(solution)/shard_map/jit(cumsum)/reduce_window_sum | solution.py:44
  73.9 0.0 copy-done.1
  73.9 0.0 copy-done.2
  74.0 1.0 fusion.9
  74.9 1.7 slice_bitcast_fusion
  76.6 1.5 stack.19
  78.2 7.5 %all-to-all-start = ((bf16[16,1,32,2048]{3,2,1,0:T(8,128)(2,1)}), bf16[16,1,32,2048]{3,2,1,0:T(8,128)(2,1)S(1)}, u32[]{:S(2)}, u32[]{:S(2)}) async-start(bf16[16,1,32,2048]{3,2,1,0:T(8,128)(2,1)} %stack.19), calls=%async_computation | async-start | bytes 4194304 | tf_op jit(solution)/shard_map/all_to_all | solution.py:80
  85.6 0.2 reduce-scatter.2.cloned.1.call-start
  85.9 32.0 %fusion.19 = (f32[32,2048]{1,0:T(8,128)S(1)}, f32[32,2048]{1,0:T(8,128)S(1)}, f32[32,2048]{1,0:T(8,128)S(1)}, f32[32,2048]{1,0:T(8,128)S(1)}) fusion(f32[32,32,2048]{2,1,0:T(8,128)} %get-tuple-element.31, f32[32,32,2048]{2,1,0:T(8,128)} %param.4, f32[]{:T(128)} %bitcast.8, f32[31,32,2048]{2,1,0:T(8,128)} %get-tuple-element.14, f32[1,32,2048]{2,1,0:T(8,128)} %copy-done, ...), kind=kLoop, calls=%fused_computation.42 | loop fusion | flops 81526784 | bytes 60555276 | tf_op jit(solution)/shard_map/reduce_sum | solution.py:54
  117.9 0.3 add_convert_fusion.1
  118.2 0.0 all-to-all-done
  118.2 3.0 %fusion.4 = f32[1,32,2048]{2,0,1:T(1,128)S(1)} fusion(bf16[16,32,2048]{2,1,0:T(8,128)(2,1)S(1)} %bitcast.27, s32[16]{0:T(128)S(1)} %copy-done.4, s32[]{:T(128)} %bitcast.9), kind=kOutput, calls=%fused_computation.15 | convolution fusion | flops 2097168 | bytes 2359364 | tf_op jit(solution)/shard_map/k,kxy->xy/dot_general | solution.py:89
  121.2 3.0 %fusion.6 = f32[1,32,2048]{2,0,1:T(1,128)S(1)} fusion(bf16[16,32,2048]{2,1,0:T(8,128)(2,1)S(1)} %bitcast.28, s32[16]{0:T(128)S(1)} %copy-done.4, s32[]{:T(128)} %bitcast.9), kind=kOutput, calls=%fused_computation.17 | convolution fusion | flops 2097168 | bytes 2359364 | tf_op jit(solution)/shard_map/k,kxy->xy/dot_general | solution.py:88
  124.2 0.1 copy.7
  124.3 0.1 copy.6
  124.4 0.1 fusion.8
  124.5 1.3 convert_multiply_fusion
  125.8 0.0 reduce-scatter.2.cloned.1.call-update
  125.8 0.4 convert_reduce_fusion
  126.2 81.8 %reduce-scatter.2.cloned.1.call-done = f32[2,3,32,128]{3,2,1,0:T(8,128)} async-done(((f32[2,3,32,2048]{3,2,1,0:T(8,128)}), f32[2,3,32,128]{3,2,1,0:T(8,128)}) %reduce-scatter.2.cloned.1.call-update) | async-done | bytes 98320 | tf_op jit(solution)/shard_map/reduce_scatter | solution.py:93
  208.0 1.6 pad_maximum_fusion.2
  (4 shorter events, 0.0 us)
Async XLA Ops:
  9.2 31.2 %collective-permute-start = (f32[32,1,2048]{2,1,0:T(1,128)S(1)}, f32[32,1,2048]{2,1,0:T(1,128)S(1)}, u32[]{:S(2)}, u32[]{:S(2)}) collective-permute-start(f32[32,1,2048]{2,1,0:T(1,128)S(1)} %get-tuple-element.19), channel_id=1, source_target_pairs={{1,0},{2,1},{3,2},{4,3},{5,4},{6,5},{7,6},{8,7},{9,8},{10,9},{11,1... | collective-permute-start | bytes 786440 | tf_op jit(solution)/shard_map/ppermute | solution.py:17
  10.5 29.9 %collective-permute-start.1 = (f32[32,1,2048]{2,1,0:T(1,128)S(1)}, f32[32,1,2048]{2,1,0:T(1,128)S(1)}, u32[]{:S(2)}, u32[]{:S(2)}) collective-permute-start(f32[32,1,2048]{2,1,0:T(1,128)S(1)} %get-tuple-element.20), channel_id=1, source_target_pairs={{0,1},{1,2},{2,3},{3,4},{4,5},{5,6},{6,7},{7,8},{8,9},{9,10},{10,1... | collective-permute-start | bytes 786440 | tf_op jit(solution)/shard_map/ppermute | solution.py:14
  13.6 12.8 %slice-start = ((s8[8388608]{0:T(1024)(128)(4,1)}), s8[4194304]{0:T(1024)(128)(4,1)S(1)}, s32[]{:S(2)}) async-start(s8[8388608]{0:T(1024)(128)(4,1)} %bitcast.25), calls=%async_computation.3 | async-start | bytes 8388608
  14.8 28.5 %copy-start = (f32[1,32,2048]{2,1,0:T(8,128)}, f32[1,32,2048]{2,1,0:T(8,128)S(1)}, u32[]{:S(2)}) copy-start(f32[1,32,2048]{2,1,0:T(8,128)S(1)} %get-tuple-element.16) | copy-start | bytes 786436
  14.8 11.6 %slice-start.1 = ((s8[8388608]{0:T(1024)(128)(4,1)}), s8[4194304]{0:T(1024)(128)(4,1)S(1)}, s32[]{:S(2)}) async-start(s8[8388608]{0:T(1024)(128)(4,1)} %bitcast.25), calls=%async_computation.4 | async-start | bytes 8388608
  26.4 7.3 %copy-start.5 = (f32[2,3]{1,0:T(2,128)S(1)}, f32[2,3]{1,0:T(2,128)}, u32[]{:S(2)}) copy-start(f32[2,3]{1,0:T(2,128)} %param.5) | copy-start | bytes 76
  26.4 7.3 %copy-start.3 = (f32[2,3]{1,0:T(2,128)S(1)}, f32[2,3]{1,0:T(2,128)}, u32[]{:S(2)}) copy-start(f32[2,3]{1,0:T(2,128)} %param.6) | copy-start | bytes 76
  26.4 11.9 %copy-start.4 = (s32[16]{0:T(128)S(1)}, s32[16]{0:T(128)}, u32[]{:S(2)}) copy-start(s32[16]{0:T(128)} %param.7) | copy-start | bytes 196
  43.3 30.7 %copy-start.1 = (f32[32,1,2048]{2,1,0:T(1,128)}, f32[32,1,2048]{2,1,0:T(1,128)S(1)}, u32[]{:S(2)}) copy-start(f32[32,1,2048]{2,1,0:T(1,128)S(1)} %get-tuple-element.17) | copy-start | bytes 786436
  43.3 30.7 %copy-start.2 = (f32[32,1,2048]{2,1,0:T(1,128)}, f32[32,1,2048]{2,1,0:T(1,128)S(1)}, u32[]{:S(2)}) copy-start(f32[32,1,2048]{2,1,0:T(1,128)S(1)} %get-tuple-element.18) | copy-start | bytes 786436
  78.2 40.0 %all-to-all-start = ((bf16[16,1,32,2048]{3,2,1,0:T(8,128)(2,1)}), bf16[16,1,32,2048]{3,2,1,0:T(8,128)(2,1)S(1)}, u32[]{:S(2)}, u32[]{:S(2)}) async-start(bf16[16,1,32,2048]{3,2,1,0:T(8,128)(2,1)} %stack.19), calls=%async_computation | async-start | bytes 4194304 | tf_op jit(solution)/shard_map/all_to_all | solution.py:80
  85.6 122.4 %reduce-scatter.2.cloned.1.call-start = ((), (), s32[]{:S(2)}) async-start(), calls=%async_computation.2 | async-start | bytes 1671168 | tf_op jit(solution)/shard_map/reduce_scatter | solution.py:93
Sparse Core Ops, SparseCore 0:
  125.9 82.0 reduce-scatter.1
